TPU v7x, 256 devices: a whole 4x4x8 slice. The times are simulated.
256 devices in a mesh: gz: 32 (over x, z_hi, core), ord: 8 (over y, z_lo).
Axes of the slice: x: 4, y: 4, z: 8 (z_hi: 4, z_lo: 2; z = z_hi * 2 + z_lo), core: 2. Of those that a mesh axis runs over, the one named last changes fastest.
Arguments:
- initial: float32 [96, 64, 128, 128], P('ord', 'gz'), may hold values from -1 to 1
- cotangent: float32 [96, 64, 128, 128], P('ord', 'gz'), may hold values from -6 to 6
- mobility: float32 [96], P('ord'), may hold values from 0.05 to 0.15
- stiffness: float32 [96], P('ord'), may hold values from 0.5 to 1
Outputs:
- adjoint_initial: float32 [96, 64, 128, 128], P('ord', 'gz')
All inputs are finite; a program needn't handle non-finite values.
Results may differ from a plain program's by a relative error of at most 0.00002.
Values sent between devices are 32-bit elements; how exact they have to be, the bound alone decides.
A program may use at most 128 MiB of HBM per device.

v0:
```python
import jax
import jax.numpy as jnp
from jax import lax
from jax.sharding import PartitionSpec as P

P_SIZE = 96


couple_scale = 2.0


def extended(block, sides, width):
    for axis, dim in sides:
        count = lax.axis_size(axis)
        forward = [(i, i + 1) for i in range(count - 1)]
        forward.append((count - 1, 0))
        backward = [(target, source) for source, target in forward]
        low = lax.ppermute(
            lax.slice_in_dim(block, block.shape[dim] - width, None, axis=dim), axis, forward
        )
        high = lax.ppermute(lax.slice_in_dim(block, 0, width, axis=dim), axis, backward)
        block = jnp.concatenate([low, block, high], axis=dim)
    return block


def inner_laplacian(values_ext):
    centre = values_ext[:, 1:-1]
    summed = values_ext[:, 2:] + values_ext[:, :-2] - 6.0 * centre
    for axis_num in (2, 3):
        summed = summed + jnp.roll(centre, 1, axis_num) + jnp.roll(centre, -1, axis_num)
    return summed


def well_slope(values, squares, coupling):
    return (
        -1.0 + 3.0 * values * values + 2.0 * coupling * squares - 6.0 * coupling * values * values
    )


def on_device(initial, cotangent, mobility, stiffness):
    order_dev = initial.shape[0]
    coupling = couple_scale / P_SIZE
    rate_col = mobility.reshape(-1, 1, 1, 1)
    stiff_col = stiffness.reshape(-1, 1, 1, 1)
    margin = 1
    joined = extended(jnp.concatenate((initial, cotangent), 0), (("gz", 1),), margin)
    field_ext = joined[:order_dev]
    adjoint_ext = joined[order_dev:]
    centre = field_ext[:, 1:-1]
    squares_first = lax.psum(jnp.sum(centre * centre, 0), "ord")
    potential = (
        -centre
        + centre * centre * centre
        + 2.0 * coupling * centre * (squares_first - centre * centre)
        - stiff_col * inner_laplacian(field_ext)
    )
    middle = centre - rate_col * potential
    scaled_ext = rate_col * adjoint_ext
    scaled = scaled_ext[:, 1:-1]
    squares_second, coupled_second = lax.psum(
        (jnp.sum(middle * middle, 0), jnp.sum(middle * scaled, 0)), "ord"
    )
    adjoint_middle = adjoint_ext[:, 1:-1] - (
        well_slope(middle, squares_second, coupling) * scaled
        + 4.0 * coupling * middle * coupled_second
        - stiff_col * inner_laplacian(scaled_ext)
    )
    scaled_middle = rate_col * adjoint_middle
    scaled_middle_ext = extended(scaled_middle, (("gz", 1),), 1)
    scaled_inner = scaled_middle_ext[:, 1:-1]
    coupled_first = lax.psum(jnp.sum(initial * scaled_inner, 0), "ord")
    return adjoint_middle - (
        well_slope(initial, squares_first, coupling) * scaled_inner
        + 4.0 * coupling * initial * coupled_first
        - stiff_col * inner_laplacian(scaled_middle_ext)
    )


def solution(mesh):
    return jax.shard_map(
        on_device,
        mesh=mesh,
        in_specs=(P("ord", "gz", None, None), P("ord", "gz", None, None), P("ord"), P("ord")),
        out_specs=P("ord", "gz", None, None),
        check_vma=False,
    )
```

profile of v0, /device:TPU:32, one launch (start us, length us, event | category | flops | bytes accessed | tf_op | source)
XLA Modules:
  0.0 313.5 jit_solution(2872398733217685041)
XLA Ops:
  6.5 0.0 all-reduce.5.cloned.1.call-start
  6.5 2.4 multiply_reduce_fusion
  9.0 0.0 copy-done.4
  9.0 0.1 constant_dynamic-update-slice_fusion
  9.1 0.0 copy-start.2
  9.1 0.0 copy-start
  9.1 1.9 fusion.47
  11.0 0.7 copy-done.2
  11.8 7.0 %collective-permute-start = (f32[24,1,128,128]{3,2,1,0:T(8,128)}, f32[24,1,128,128]{3,2,1,0:T(8,128)S(1)}, u32[]{:S(2)}, u32[]{:S(2)}) collective-permute-start(f32[24,1,128,128]{3,2,1,0:T(8,128)} %get-tuple-element.22), channel_id=1, source_target_pairs={{8,0},{16,8},{24,16},{32,24},{40,32},{48,40},{56,48},{64,56},{72,6... | collective-permute-start | bytes 4718600 | tf_op jit(solution)/shard_map/ppermute | solution.py:21
  18.8 0.0 collective-permute-start.1
  18.8 0.0 all-reduce.5.cloned.1.call-update
  18.8 0.0 all-reduce.9.cloned.1.call-start
  18.9 2.0 fusion.54
  20.8 2.2 fusion.55
  23.0 2.3 fusion.56
  25.3 82.3 %all-reduce.5.cloned.1.call-done = f32[2,128,128]{2,1,0:T(8,128)} async-done(((f32[2,128,128]{2,1,0:T(8,128)}), f32[2,128,128]{2,1,0:T(8,128)}) %all-reduce.5.cloned.1.call-update) | async-done | bytes 131088 | tf_op jit(solution)/shard_map/psum | solution.py:50
  107.6 0.9 broadcast_multiply_fusion.3
  108.5 0.0 collective-permute-done
  108.6 0.0 collective-permute-done.1
  108.6 2.1 fusion
  110.7 2.0 fusion.44
  112.7 2.2 fusion.45
  114.9 0.5 copy-done.1
  115.4 1.0 copy-done.9
  116.4 0.5 copy-done.10
  116.8 1.1 copy-done.3
  117.9 0.4 copy-done.5
  118.3 0.4 copy-done.6
  118.8 4.8 %multiply_reduce_fusion.3 = (f32[2,128,128]{2,1,0:T(8,128)}, f32[2,128,128]{2,1,0:T(8,128)}, f32[12,2,128,128]{3,2,1,0:T(8,128)}) fusion(f32[12,4,128,128]{3,2,1,0:T(8,128)S(1)} %fusion, f32[12,2,128,128]{3,2,1,0:T(8,128)S(1)} %copy-done, f32[12,2,128,1]{3,2,1,0:T(8,128)S(1)} %copy-done.8, f32[12,2,128,127]{3,2,1,0:T(8,128)S(1)} %copy-done.10, ...), kind=kLoop, calls=%fused_computation.57 | loop fusion | flops 11337728 | bytes 17694816 | tf_op jit(solution)/shard_map/reduce_sum | solution.py:61
  123.6 0.0 all-reduce.9.cloned.1.call-update
  123.6 0.0 all-reduce.7.cloned.1.call-start
  123.7 4.3 %fusion.46 = (f32[12,2,128,127]{3,2,1,0:T(8,128)}, f32[12,2,128,127]{3,2,1,0:T(8,128)}) fusion(f32[12,4,128,128]{3,2,1,0:T(8,128)} %copy-done.1), kind=kLoop, calls=%fused_computation.68 | loop fusion | bytes 6242304 | tf_op jit(solution)/shard_map/jit(_roll_static)/slice | solution.py:30
  127.9 1.0 fusion.43
  128.9 72.7 %all-reduce.9.cloned.1.call-done = (f32[2,128,128]{2,1,0:T(8,128)}, f32[2,128,128]{2,1,0:T(8,128)}) async-done(((f32[2,128,128]{2,1,0:T(8,128)}, f32[2,128,128]{2,1,0:T(8,128)}), (f32[2,128,128]{2,1,0:T(8,128)}, f32[2,128,128]{2,1,0:T(8,128)})) %all-reduce.9.cloned.1.call-update) | async-done | bytes 262160 | tf_op jit(solution)/shard_map/psum | solution.py:60
  201.7 1.0 broadcast_multiply_fusion.2
  202.6 8.8 %multiply_reduce_fusion.1 = (f32[2,128,128]{2,1,0:T(8,128)}, f32[12,2,128,128]{3,2,1,0:T(8,128)S(1)}, f32[12,2,128,128]{3,2,1,0:T(8,128)}) fusion(f32[12,2,128,128]{3,2,1,0:T(8,128)S(1)} %copy-done, f32[12]{0:T(128)S(1)} %copy-done.12, f32[12,2,128,128]{3,2,1,0:T(8,128)} %param.5, f32[12,2,128,1]{3,2,1,0:T(8,128)} %get-tuple-element.18, ...), kind=kLoop, calls=%fused_computation.55 | loop fusion | flops 10584064 | bytes 19267680 | tf_op jit(solution)/shard_map/reduce_sum | solution.py:71
  211.5 2.2 fusion.48
  213.7 2.2 fusion.49
  215.9 1.3 fusion.52
  217.2 0.5 collective-permute-start.2
  217.7 0.0 collective-permute-start.3
  217.7 0.0 all-reduce.7.cloned.1.call-update
  217.7 2.1 fusion.50
  219.8 79.8 %all-reduce.7.cloned.1.call-done = f32[2,128,128]{2,1,0:T(8,128)} async-done(((f32[2,128,128]{2,1,0:T(8,128)}), f32[2,128,128]{2,1,0:T(8,128)}) %all-reduce.7.cloned.1.call-update) | async-done | bytes 131088 | tf_op jit(solution)/shard_map/psum | solution.py:71
  299.6 0.9 broadcast_multiply_fusion.1
  300.5 0.0 collective-permute-done.2
  300.5 0.0 collective-permute-done.3
  300.5 6.4 %fusion.20 = f32[12,2,128,128]{3,2,1,0:T(8,128)} fusion(f32[12,2,128,128]{3,2,1,0:T(8,128)} %get-tuple-element.11, f32[12,2,128,128]{3,2,1,0:T(8,128)S(1)} %get-tuple-element.10, f32[12,2,128,128]{3,2,1,0:T(8,128)S(1)} %copy-done, f32[12,1,128,128]{3,2,1,0:T(8,128)} %collective-permute-done.3, f32[12,1,128,128]{3,2,1,0:T(8,128)} %collective-permute-done.2, ...), kind=kLoop, calls=%fused_computation.29 | loop fusion | flops 10223616 | bytes 14417968 | tf_op jit(solution)/shard_map/sub | solution.py:72
  (20 shorter events, 0.1 us)
Async XLA Ops:
  6.5 2.4 copy-start.4
  6.5 101.1 %all-reduce.5.cloned.1.call-start = ((), (), s32[]{:S(2)}) async-start(), calls=%async_computation | async-start | bytes 262144 | tf_op jit(solution)/shard_map/psum | solution.py:50
  9.1 2.7 copy-start.2
  9.1 9.8 %copy-start = (f32[12,2,128,128]{3,2,1,0:T(8,128)S(1)}, f32[12,2,128,128]{3,2,1,0:T(8,128)}, u32[]{:S(2)}) copy-start(f32[12,2,128,128]{3,2,1,0:T(8,128)} %param.4) | copy-start | bytes 4718596
  11.8 96.8 %collective-permute-start = (f32[24,1,128,128]{3,2,1,0:T(8,128)}, f32[24,1,128,128]{3,2,1,0:T(8,128)S(1)}, u32[]{:S(2)}, u32[]{:S(2)}) collective-permute-start(f32[24,1,128,128]{3,2,1,0:T(8,128)} %get-tuple-element.22), channel_id=1, source_target_pairs={{8,0},{16,8},{24,16},{32,24},{40,32},{48,40},{56,48},{64,56},{72,6... | collective-permute-start | bytes 4718600 | tf_op jit(solution)/shard_map/ppermute | solution.py:21
  18.8 89.8 %collective-permute-start.1 = (f32[24,1,128,128]{3,2,1,0:T(8,128)}, f32[24,1,128,128]{3,2,1,0:T(8,128)}, u32[]{:S(2)}, u32[]{:S(2)}) collective-permute-start(f32[24,1,128,128]{3,2,1,0:T(8,128)} %get-tuple-element.21), channel_id=1, source_target_pairs={{0,8},{8,16},{16,24},{24,32},{32,40},{40,48},{48,56},{56,64},{64,7... | collective-permute-start | bytes 4718600 | tf_op jit(solution)/shard_map/ppermute | solution.py:18
  18.8 182.8 %all-reduce.9.cloned.1.call-start = ((), (), s32[]{:S(2)}) async-start(), calls=%async_computation.2 | async-start | bytes 524288 | tf_op jit(solution)/shard_map/psum | solution.py:60
  23.0 85.5 %copy-start.12 = (f32[12]{0:T(128)S(1)}, f32[12]{0:T(128)}, u32[]{:S(2)}) copy-start(f32[12]{0:T(128)} %param.6) | copy-start | bytes 148
  108.6 6.8 %copy-start.11 = (f32[2,128,128]{2,1,0:T(8,128)S(1)}, f32[2,128,128]{2,1,0:T(8,128)}, u32[]{:S(2)}) copy-start(f32[2,128,128]{2,1,0:T(8,128)} %all-reduce.5.cloned.1.call-done) | copy-start | bytes 393220
  110.6 4.7 %copy-start.1 = (f32[12,4,128,128]{3,2,1,0:T(8,128)}, f32[12,4,128,128]{3,2,1,0:T(8,128)S(1)}, u32[]{:S(2)}) copy-start(f32[12,4,128,128]{3,2,1,0:T(8,128)S(1)} %fusion) | copy-start | bytes 9437188
  110.7 4.7 %copy-start.7 = (f32[12,2,128,1]{3,2,1,0:T(8,128)S(1)}, f32[12,2,128,1]{3,2,1,0:T(8,128)}, u32[]{:S(2)}) copy-start(f32[12,2,128,1]{3,2,1,0:T(8,128)} %get-tuple-element.39) | copy-start | bytes 36868
  110.7 4.7 %copy-start.8 = (f32[12,2,128,1]{3,2,1,0:T(8,128)S(1)}, f32[12,2,128,1]{3,2,1,0:T(8,128)}, u32[]{:S(2)}) copy-start(f32[12,2,128,1]{3,2,1,0:T(8,128)} %get-tuple-element.40) | copy-start | bytes 36868
  110.7 5.7 %copy-start.9 = (f32[12,2,128,127]{3,2,1,0:T(8,128)S(1)}, f32[12,2,128,127]{3,2,1,0:T(8,128)}, u32[]{:S(2)}) copy-start(f32[12,2,128,127]{3,2,1,0:T(8,128)} %get-tuple-element.41) | copy-start | bytes 4681732
  110.7 6.2 %copy-start.10 = (f32[12,2,128,127]{3,2,1,0:T(8,128)S(1)}, f32[12,2,128,127]{3,2,1,0:T(8,128)}, u32[]{:S(2)}) copy-start(f32[12,2,128,127]{3,2,1,0:T(8,128)} %get-tuple-element.42) | copy-start | bytes 4681732
  112.7 5.2 %copy-start.3 = (f32[24,2,128,128]{3,2,1,0:T(8,128)S(1)}, f32[24,2,128,128]{3,2,1,0:T(8,128)}, u32[]{:S(2)}) copy-start(f32[24,2,128,128]{3,2,1,0:T(8,128)} %copy-done.2) | copy-start | bytes 9437188
  112.7 5.7 %copy-start.5 = (f32[12,2,127,128]{3,2,1,0:T(8,128)S(1)}, f32[12,2,127,128]{3,2,1,0:T(8,128)}, u32[]{:S(2)}) copy-start(f32[12,2,127,128]{3,2,1,0:T(8,128)} %get-tuple-element.37) | copy-start | bytes 4681732
  112.7 6.1 %copy-start.6 = (f32[12,2,127,128]{3,2,1,0:T(8,128)S(1)}, f32[12,2,127,128]{3,2,1,0:T(8,128)}, u32[]{:S(2)}) copy-start(f32[12,2,127,128]{3,2,1,0:T(8,128)} %get-tuple-element.38) | copy-start | bytes 4681732
  112.7 6.1 %copy-start.13 = (f32[12]{0:T(128)S(1)}, f32[12]{0:T(128)}, u32[]{:S(2)}) copy-start(f32[12]{0:T(128)} %param.7) | copy-start | bytes 148
  123.6 176.0 %all-reduce.7.cloned.1.call-start = ((), (), s32[]{:S(2)}) async-start(), calls=%async_computation.1 | async-start | bytes 262144 | tf_op jit(solution)/shard_map/psum | solution.py:71
  217.2 83.3 %collective-permute-start.2 = (f32[12,1,128,128]{3,2,1,0:T(8,128)}, f32[12,1,128,128]{3,2,1,0:T(8,128)}, u32[]{:S(2)}, u32[]{:S(2)}) collective-permute-start(f32[12,1,128,128]{3,2,1,0:T(8,128)} %get-tuple-element.31), channel_id=1, source_target_pairs={{8,0},{16,8},{24,16},{32,24},{40,32},{48,40},{56,48},{64,56},{72,6... | collective-permute-start | bytes 2359304 | tf_op jit(solution)/shard_map/ppermute | solution.py:21
  217.7 82.8 %collective-permute-start.3 = (f32[12,1,128,128]{3,2,1,0:T(8,128)}, f32[12,1,128,128]{3,2,1,0:T(8,128)}, u32[]{:S(2)}, u32[]{:S(2)}) collective-permute-start(f32[12,1,128,128]{3,2,1,0:T(8,128)} %get-tuple-element.32), channel_id=1, source_target_pairs={{0,8},{8,16},{16,24},{24,32},{32,40},{40,48},{48,56},{56,64},{64,7... | collective-permute-start | bytes 2359304 | tf_op jit(solution)/shard_map/ppermute | solution.py:18
Sparse Core Ops, SparseCore 0:
  18.9 88.6 all-reduce.4
  123.7 77.8 all-reduce.8
  217.8 81.6 all-reduce.6
where the time goes:
time: 317 us; the launch traced here: 313 us
  waiting for transfers between devices  235 us (74%)
  local copies, waits for them, and re-layouts  30.3 us (10%)
  other arithmetic  27.4 us (9%)
  between operations  13.3 us (4%)
  starting transfers between devices  7.65 us (2%)
    psum x1, waiting for transfers between devices, on_device(): squares_first = lax.psum(jnp.sum(centre * centre, 0), 'ord')  82.3 us
    psum x1, waiting for transfers between devices, on_device(): coupled_first = lax.psum(jnp.sum(initial * scaled_inner, 0), 'ord')  79.8 us
    psum x1, waiting for transfers between devices, on_device(): lax.psum((jnp.sum(middle * middle, 0), jnp.sum(middle * scaled, 0)), 'ord')  72.7 us
    slice x8, local copies, waits for them, and re-layouts, inner_laplacian(): jnp.roll(centre, 1, axis_num)  15.9 us
    reduce_sum x1, other arithmetic, on_device(): coupled_first = lax.psum(jnp.sum(initial * scaled_inner, 0), 'ord')  8.83 us
    ppermute x2, starting transfers between devices, extended(): lax.ppermute(lax.slice_in_dim(block, 0, width, axis=dim), axis, backward)  7.56 us
    slice x4, local copies, waits for them, and re-layouts, inner_laplacian(): jnp.roll(centre, -1, axis_num)  6.48 us
    sub x1, other arithmetic, on_device(): adjoint_middle - (well_slope(initial, squares_first, coupling) * scaled_i...  6.4 us
  transfers between devices with their start and end apart: 7, of which 3 were waited for; matrix products, arithmetic and copies ran while one was open for 5% of the time, Pallas kernels for 0%

commit v1 on v0

v1 whole, which is shorter than its diff:
```python
import functools

import jax
import jax.numpy as jnp
from jax import lax
from jax.experimental import pallas as pl
from jax.experimental.pallas import tpu as pltpu
from jax.sharding import PartitionSpec as P

P_SIZE = 96
COUPLE = 2.0 / P_SIZE
CUBE = 3.0 - 6.0 * COUPLE
MESH = pl.DeviceIdType.MESH
HALVES = 2


def flat_laplacian(plane, other):
    rows, cols = plane.shape
    side = pltpu.roll(plane, 1, 0) + pltpu.roll(plane, rows - 1, 0)
    side = side + (pltpu.roll(plane, 1, 1) + pltpu.roll(plane, cols - 1, 1))
    return side + (other - 6.0 * plane)


def kernel(
    n_gz, n_y,
    u_hbm, a_hbm, rate_hbm, stiff_hbm,
    part, w_halo,
    rate, stiff, u, a, mid, adj, w, u_halo, a_halo, partial, parts, half_sum, half_in, total, result,
    load_sem, far_send, far_recv, near_send, near_recv,
    in_send, in_recv, mid_send, mid_recv, out_send, out_recv, store_sem,
):
    order, planes, nx, ny = u.shape
    gz, ord_ = lax.axis_index("gz"), lax.axis_index("ord")
    core, y, zl = lax.rem(gz, 2), ord_ // 2, lax.rem(ord_, 2)
    sibling = gz + 1 - 2 * core
    chip = gz - core
    far = lax.rem(jnp.where(core == 1, gz + 1, gz + n_gz - 1), n_gz)
    far_plane, near_plane = core, 1 - core
    reducer = core == zl
    half_rows = nx // HALVES

    def at(gz_=None, y_=None, zl_=None):
        y_ = y if y_ is None else y_
        zl_ = zl if zl_ is None else zl_
        return {"gz": gz if gz_ is None else gz_, "ord": 2 * y_ + zl_}

    loads = [
        pltpu.make_async_copy(u_hbm, u, load_sem.at[0]),
        pltpu.make_async_copy(a_hbm, a, load_sem.at[1]),
        pltpu.make_async_copy(rate_hbm, rate, load_sem.at[2]),
        pltpu.make_async_copy(stiff_hbm, stiff, load_sem.at[3]),
    ]
    for copy in loads:
        copy.start()

    barrier = pltpu.get_barrier_semaphore()
    peers = [at(far), at(sibling, zl_=1 - zl), at(sibling)]
    for step in range(1, n_y):
        for c in range(2):
            peers.append(at(chip + c, lax.rem(y + step, n_y)))
    for peer in peers:
        pl.semaphore_signal(barrier, inc=1, device_id=peer, device_id_type=MESH)
    pl.semaphore_wait(barrier, len(peers))

    def halo(index, src, dst, far_side, rows):
        mine = far_plane if far_side else near_plane
        theirs = 1 - mine
        return pltpu.make_async_remote_copy(
            src_ref=src.at[:, mine, rows],
            dst_ref=dst.at[:, theirs, rows],
            send_sem=(far_send if far_side else near_send).at[index],
            recv_sem=(far_recv if far_side else near_recv).at[index],
            device_id=at(far if far_side else sibling),
            device_id_type=MESH,
        )

    def half(h):
        return pl.ds(h * half_rows, half_rows)

    u_far = [halo(h, u_hbm, u_halo, True, half(h)) for h in range(HALVES)]
    a_far = [halo(HALVES + h, a_hbm, a_halo, True, half(h)) for h in range(HALVES)]
    w_far = [halo(2 * HALVES + h, w, w_halo, True, half(h)) for h in range(HALVES)]
    u_near = halo(0, u_hbm, u_halo, False, pl.ds(0, nx))
    a_near = halo(1, a_hbm, a_halo, False, pl.ds(0, nx))
    w_near = [halo(2 + h, w, w_halo, False, half(h)) for h in range(HALVES)]
    for copy in u_far + [u_near] + a_far:
        copy.start()

    class Total:
        def __init__(self, call, sums, first, rows):
            self.call, self.sums, self.first, self.quarter = call, sums, first, rows // n_y

        def rows(self, y_):
            return pl.ds(pl.multiple_of(self.first + y_ * self.quarter, 8), self.quarter)

        def block(self, ref, *lead):
            return ref.at[(*lead, pl.ds(0, self.sums), slice(None), pl.ds(0, self.quarter))]

        def source(self, y_):
            return partial.at[pl.ds(0, self.sums), :, self.rows(y_)]

        def gather(self, step, from_core):
            to = lax.rem(y + step, n_y)
            return pltpu.make_async_remote_copy(
                src_ref=self.source(to),
                dst_ref=self.block(parts, self.call, from_core, step),
                send_sem=in_send.at[self.call, step],
                recv_sem=in_recv.at[self.call, from_core, step],
                device_id=at(chip + zl, to),
                device_id_type=MESH,
            )

        def swap(self):
            return pltpu.make_async_remote_copy(
                src_ref=self.block(half_sum, self.call, slice(None)),
                dst_ref=self.block(half_in, self.call, slice(None)),
                send_sem=mid_send.at[self.call],
                recv_sem=mid_recv.at[self.call],
                device_id=at(sibling, zl_=1 - zl),
                device_id_type=MESH,
            )

        def spread(self, step, to_core, from_step=None):
            return pltpu.make_async_remote_copy(
                src_ref=self.block(total, self.call, to_core),
                dst_ref=result.at[self.call, pl.ds(0, self.sums), :, self.rows(y)],
                send_sem=out_send.at[self.call, to_core, step],
                recv_sem=out_recv.at[self.call, step],
                device_id=at(chip + to_core, lax.rem(y + step, n_y)),
                device_id_type=MESH,
            )

        def arriving(self, step):
            from_ = lax.rem(y + n_y - step, n_y)
            return pltpu.make_async_remote_copy(
                src_ref=self.block(total, self.call, core),
                dst_ref=result.at[self.call, pl.ds(0, self.sums), :, self.rows(from_)],
                send_sem=out_send.at[self.call, core, step],
                recv_sem=out_recv.at[self.call, step],
                device_id=at(),
                device_id_type=MESH,
            )

        def send(self):
            for step in range(1, n_y):
                self.gather(step, core).start()

            @pl.when(jnp.logical_not(reducer))
            def _():
                self.gather(0, core).start()

        def reduce(self):
            @pl.when(reducer)
            def _():
                self.block(parts, self.call, core, 0)[...] = self.source(y)[...]
                self.gather(0, 1 - core).wait_recv()
                for step in range(1, n_y):
                    for c in range(2):
                        self.gather(step, c).wait_recv()
                for c in range(2):
                    block = self.block(parts, self.call, c, 0)[...]
                    for step in range(1, n_y):
                        block = block + self.block(parts, self.call, c, step)[...]
                    self.block(half_sum, self.call, c)[...] = block
                self.swap().start()

        def finish(self):
            @pl.when(reducer)
            def _():
                self.swap().wait_recv()
                for c in range(2):
                    self.block(total, self.call, c)[...] = (
                        self.block(half_sum, self.call, c)[...] + self.block(half_in, self.call, c)[...]
                    )
                for step in range(1, n_y):
                    for c in range(2):
                        self.spread(step, c).start()
                self.spread(0, 1 - core).start()
                result[self.call, pl.ds(0, self.sums), :, self.rows(y)] = self.block(total, self.call, core)[...]

        def arrive(self):
            for step in range(1, n_y):
                self.arriving(step).wait_recv()

            @pl.when(jnp.logical_not(reducer))
            def _():
                self.arriving(0).wait_recv()

        def drain(self):
            for step in range(1, n_y):
                self.gather(step, core).wait_send()

            @pl.when(jnp.logical_not(reducer))
            def _():
                self.gather(0, core).wait_send()

            @pl.when(reducer)
            def _():
                self.swap().wait_send()
                for step in range(1, n_y):
                    for c in range(2):
                        self.spread(step, c).wait_send()
                self.spread(0, 1 - core).wait_send()

    squares_first = Total(0, 1, 0, nx)
    second = [Total(1 + h, 2, h * half_rows, half_rows) for h in range(HALVES)]
    coupled_first = [Total(1 + HALVES + h, 1, h * half_rows, half_rows) for h in range(HALVES)]

    loads[0].wait()
    for z in range(planes):

        def add_square(p, acc):
            value = u[p, z]
            return acc + value * value

        partial[0, z] = lax.fori_loop(0, order, add_square, jnp.zeros((nx, ny), jnp.float32))
    squares_first.send()
    a_near.start()

    loads[2].wait()
    loads[3].wait()

    def own_middle(i, _):
        p, z = i // planes, lax.rem(i, planes)
        value = u[p, z]
        m, k = rate[p], stiff[p]
        slope = (1.0 + m) - (m * (1.0 - 2.0 * COUPLE)) * (value * value)
        mid[p, z] = value * slope + (m * k) * flat_laplacian(value, u[p, 1 - z])
        return 0

    lax.fori_loop(0, order * planes, own_middle, 0)
    squares_first.reduce()

    loads[1].wait()

    def own_adjoint(i, _):
        p, z = i // planes, lax.rem(i, planes)
        value = a[p, z]
        m, k = rate[p], stiff[p]
        adj[p, z] = (1.0 + m) * value + (m * k) * flat_laplacian(value, a[p, 1 - z])
        return 0

    lax.fori_loop(0, order * planes, own_adjoint, 0)
    squares_first.finish()
    squares_first.arrive()
    squares_first.drain()

    u_near.wait_recv()
    for h in range(HALVES):
        rows = half(h)
        u_far[h].wait_recv()
        for z in range(planes):
            weight = (2.0 * COUPLE) * result[0, 0, z, rows]

            def middle(p, carry):
                squares, coupled = carry
                m, k = rate[p], stiff[p]
                value = mid[p, z, rows] - m * (u[p, z, rows] * weight)
                value = value + (m * k) * u_halo[p, z, rows]
                mid[p, z, rows] = value
                return squares + value * value, coupled + value * (m * a[p, z, rows])

            zero = jnp.zeros((half_rows, ny), jnp.float32)
            squares, coupled = lax.fori_loop(0, order, middle, (zero, zero))
            partial[0, z, rows] = squares
            partial[1, z, rows] = coupled
        second[h].send()
        second[h].reduce()
        second[h].finish()
        second[h].arrive()
        second[h].drain()

    a_near.wait_recv()
    for h in range(HALVES):
        rows = half(h)
        a_far[h].wait_recv()
        for z in range(planes):
            weight = (2.0 * COUPLE) * result[1 + h, 0, z, rows]
            pull = (4.0 * COUPLE) * result[1 + h, 1, z, rows]

            def adjoint(p, acc):
                m, k = rate[p], stiff[p]
                field = mid[p, z, rows]
                value = adj[p, z, rows] - (m * a[p, z, rows]) * (CUBE * (field * field) + weight)
                value = value - field * pull + (m * k) * a_halo[p, z, rows]
                adj[p, z, rows] = value
                scaled = m * value
                w[p, z, rows] = scaled
                return acc + u[p, z, rows] * scaled

            partial[0, z, rows] = lax.fori_loop(
                0, order, adjoint, jnp.zeros((half_rows, ny), jnp.float32)
            )
        w_far[h].start()
        w_near[h].start()
        coupled_first[h].send()

    for h in range(HALVES):
        coupled_first[h].reduce()

    def own_result(i, _):
        p, z = i // planes, lax.rem(i, planes)
        value, scaled = u[p, z], w[p, z]
        slope = CUBE * (value * value) + (2.0 * COUPLE) * result[0, 0, z]
        local = adj[p, z] + scaled - scaled * slope
        adj[p, z] = local + stiff[p] * flat_laplacian(scaled, w[p, 1 - z])
        return 0

    lax.fori_loop(0, order * planes, own_result, 0)
    for h in range(HALVES):
        coupled_first[h].finish()
    for h in range(HALVES):
        rows = half(h)
        coupled_first[h].arrive()
        for z in range(planes):
            pull = (4.0 * COUPLE) * result[1 + HALVES + h, 0, z, rows]

            def couple(p, _):
                adj[p, z, rows] = adj[p, z, rows] - u[p, z, rows] * pull
                return 0

            lax.fori_loop(0, order, couple, 0)
    store = pltpu.make_async_copy(adj, part, store_sem)
    store.start()
    for h in range(HALVES):
        coupled_first[h].drain()
    for copy in u_far + a_far + [u_near, a_near]:
        copy.wait_send()
    for copy in w_near + w_far:
        copy.wait()
    store.wait()


def on_device(n_gz, n_ord, initial, cotangent, mobility, stiffness):
    shape = initial.shape
    order, planes, nx, ny = shape
    n_y = n_ord // 2
    calls = 1 + 2 * HALVES
    f32 = jnp.float32
    field = jax.ShapeDtypeStruct(shape, f32)
    quarter = nx // n_y
    part, w_halo = pl.pallas_call(
        functools.partial(kernel, n_gz, n_y),
        out_shape=(field, field),
        in_specs=[pl.BlockSpec(memory_space=pltpu.HBM)] * 4,
        out_specs=[pl.BlockSpec(memory_space=pl.ANY)] * 2,
        scratch_shapes=[pltpu.SMEM((order,), f32)] * 2
        + [pltpu.VMEM(shape, f32)] * 7
        + [
            pltpu.VMEM((2, planes, nx, ny), f32),
            pltpu.VMEM((calls, 2, n_y, 2, planes, quarter, ny), f32),
            pltpu.VMEM((calls, 2, 2, planes, quarter, ny), f32),
            pltpu.VMEM((calls, 2, 2, planes, quarter, ny), f32),
            pltpu.VMEM((calls, 2, 2, planes, quarter, ny), f32),
            pltpu.VMEM((calls, 2, planes, nx, ny), f32),
            pltpu.SemaphoreType.DMA((4,)),
            pltpu.SemaphoreType.DMA((3 * HALVES,)),
            pltpu.SemaphoreType.DMA((3 * HALVES,)),
            pltpu.SemaphoreType.DMA((2 + HALVES,)),
            pltpu.SemaphoreType.DMA((2 + HALVES,)),
            pltpu.SemaphoreType.DMA((calls, n_y)),
            pltpu.SemaphoreType.DMA((calls, 2, n_y)),
            pltpu.SemaphoreType.DMA((calls,)),
            pltpu.SemaphoreType.DMA((calls,)),
            pltpu.SemaphoreType.DMA((calls, 2, n_y)),
            pltpu.SemaphoreType.DMA((calls, n_y)),
            pltpu.SemaphoreType.DMA,
        ],
        compiler_params=pltpu.CompilerParams(
            collective_id=0, has_side_effects=True, vmem_limit_bytes=32 << 20
        ),
        name="adjoint_steps",
    )(*(pltpu.with_memory_space_constraint(x, pltpu.HBM) for x in (initial, cotangent, mobility, stiffness)))
    return part + stiffness.reshape(-1, 1, 1, 1) * w_halo


def solution(mesh):
    return jax.shard_map(
        functools.partial(on_device, mesh.shape["gz"], mesh.shape["ord"]),
        mesh=mesh,
        in_specs=(P("ord", "gz", None, None), P("ord", "gz", None, None), P("ord"), P("ord")),
        out_specs=P("ord", "gz", None, None),
        check_vma=False,
    )
```

time: 317 us -> 77.9 us (0.25); the launches traced: 313 us -> 77.8 us
  waiting for transfers between devices: 235 us -> 0 us
  Pallas kernels: 0 us -> 76.3 us
  local copies, waits for them, and re-layouts: 30.3 us -> 0.01 us
  other arithmetic: 27.4 us -> 1.49 us
  between operations: 13.3 us -> 0.02 us
  starting transfers between devices: 7.65 us -> 0 us
    psum x3 -> x0, waiting for transfers between devices: 235 us -> none  [the longest x1 82.3 us: on_device(): squares_first = lax.psum(jnp.sum(centre * centre, 0), 'ord')]
    pallas_call x0 -> x1, Pallas kernels: none -> 76.3 us  [on_device(): pl.pallas_call(functools.partial(kernel, n_gz, n_y), out_shape=(field, fi...]
    slice x14 -> x0, local copies, waits for them, and re-layouts: 25.6 us -> none  [the longest x8 15.9 us: inner_laplacian(): jnp.roll(centre, 1, axis_num)]
    reduce_sum x3 -> x0, other arithmetic: 16.1 us -> none  [the longest x1 8.83 us: on_device(): coupled_first = lax.psum(jnp.sum(initial * scaled_inner, 0), 'ord')]
    ppermute x4 -> x0, starting transfers between devices: 7.56 us -> none  [the longest x2 7.56 us: extended(): lax.ppermute(lax.slice_in_dim(block, 0, width, axis=dim), axis, backward)]
    sub x1 -> x0, other arithmetic: 6.4 us -> none  [on_device(): adjoint_middle - (well_slope(initial, squares_first, coupling) * scaled_i...]
    mul x4 -> x0, other arithmetic: 4.88 us -> none  [the longest x1 2.06 us: on_device(): scaled_ext = rate_col * adjoint_ext]
    unnamed x28 -> x2, local copies, waits for them, and re-layouts: 4.65 us -> 0.01 us
  transfers between devices with their start and end apart: 7 -> 0, of which waited for: 3 -> 0; matrix products, arithmetic and copies ran while one was open for 5% -> 0% of each run, Pallas kernels for 0% -> 0%
where the time goes in v1:
time: 77.9 us; the launch traced here: 77.8 us
  Pallas kernels  76.3 us (98%)
  other arithmetic  1.49 us (2%)
    pallas_call x1, Pallas kernels, on_device(): pl.pallas_call(functools.partial(kernel, n_gz, n_y), out_shape=(field, fi...  76.3 us

profile of v1, /device:TPU:32, one launch (start us, length us, event | category | flops | bytes accessed | tf_op | source)
XLA Modules:
  0.0 77.8 jit_solution(10747054295834964601)
XLA Ops:
  0.0 0.0 copy-start
  0.0 76.3 %adjoint_steps.1 = (f32[12,2,128,128]{3,2,1,0:T(8,128)S(1)}, f32[12,2,128,128]{3,2,1,0:T(8,128)S(1)}) custom-call(f32[12,2,128,128]{3,2,1,0:T(8,128)} %u_hbm.1, f32[12,2,128,128]{3,2,1,0:T(8,128)} %a_hbm.1, f32[12]{0:T(128)} %rate_hbm.1, f32[12]{0:T(128)} %stiff_hbm.1), custom_call_target="tpu_custom_call" | custom-call | tf_op jit(solution)/shard_map/adjoint_steps/pallas_call | solution.py:342
  76.3 0.0 copy-done
  76.3 1.5 %multiply_add_fusion = f32[12,2,128,128]{3,2,1,0:T(8,128)} fusion(f32[12,2,128,128]{3,2,1,0:T(8,128)S(1)} %get-tuple-element.7, f32[12,2,128,128]{3,2,1,0:T(8,128)S(1)} %get-tuple-element.8, f32[12]{0:T(128)S(1)} %copy-done), kind=kLoop, calls=%fused_computation | loop fusion | flops 786432 | bytes 4718640 | tf_op jit(solution)/shard_map/add | solution.py:374
Async XLA Ops:
  0.0 76.3 %copy-start = (f32[12]{0:T(128)S(1)}, f32[12]{0:T(128)}, u32[]{:S(2)}) copy-start(f32[12]{0:T(128)} %stiff_hbm.1) | copy-start | bytes 148

commit v2 on v1

--- a/solution.py
+++ b/solution.py
@@ -12,6 +12,7 @@
 CUBE = 3.0 - 6.0 * COUPLE
 MESH = pl.DeviceIdType.MESH
 HALVES = 2
+SPREAD = (2, 1, 3)
 
 
 def flat_laplacian(plane, other):
@@ -90,117 +91,108 @@
         def __init__(self, call, sums, first, rows):
             self.call, self.sums, self.first, self.quarter = call, sums, first, rows // n_y
 
-        def rows(self, y_):
-            return pl.ds(pl.multiple_of(self.first + y_ * self.quarter, 8), self.quarter)
-
-        def block(self, ref, *lead):
-            return ref.at[(*lead, pl.ds(0, self.sums), slice(None), pl.ds(0, self.quarter))]
-
-        def source(self, y_):
-            return partial.at[pl.ds(0, self.sums), :, self.rows(y_)]
-
-        def gather(self, step, from_core):
+        def rows(self, y_, count=1):
+            return pl.ds(pl.multiple_of(self.first + y_ * self.quarter, 8), count * self.quarter)
+
+        def block(self, ref, slot):
+            return ref.at[self.call, slot, pl.ds(0, self.sums), :, pl.ds(0, self.quarter)]
+
+        def source(self, y_, count=1):
+            return partial.at[pl.ds(0, self.sums), :, self.rows(y_, count)]
+
+        def target(self, y_, count=1):
+            return result.at[self.call, pl.ds(0, self.sums), :, self.rows(y_, count)]
+
+        def wait(self, ref, sem, arrival):
+            copy = pltpu.make_async_remote_copy(ref, ref, sem, sem, device_id=at(sibling), device_id_type=MESH)
+            (copy.wait_recv if arrival else copy.wait_send)()
+
+        def seven(self):
+            return self.block(parts, pl.ds(1, 2 * n_y - 1))
+
+        def gather(self, step):
             to = lax.rem(y + step, n_y)
             return pltpu.make_async_remote_copy(
                 src_ref=self.source(to),
-                dst_ref=self.block(parts, self.call, from_core, step),
-                send_sem=in_send.at[self.call, step],
-                recv_sem=in_recv.at[self.call, from_core, step],
+                dst_ref=self.block(parts, jnp.where(reducer, 0, n_y) + step),
+                send_sem=in_send.at[self.call],
+                recv_sem=in_recv.at[self.call],
                 device_id=at(chip + zl, to),
                 device_id_type=MESH,
             )
 
         def swap(self):
             return pltpu.make_async_remote_copy(
-                src_ref=self.block(half_sum, self.call, slice(None)),
-                dst_ref=self.block(half_in, self.call, slice(None)),
+                src_ref=self.block(half_sum, slice(None)),
+                dst_ref=self.block(half_in, slice(None)),
                 send_sem=mid_send.at[self.call],
                 recv_sem=mid_recv.at[self.call],
                 device_id=at(sibling, zl_=1 - zl),
                 device_id_type=MESH,
             )
 
-        def spread(self, step, to_core, from_step=None):
+        def spread(self, step, group):
             return pltpu.make_async_remote_copy(
-                src_ref=self.block(total, self.call, to_core),
-                dst_ref=result.at[self.call, pl.ds(0, self.sums), :, self.rows(y)],
-                send_sem=out_send.at[self.call, to_core, step],
-                recv_sem=out_recv.at[self.call, step],
-                device_id=at(chip + to_core, lax.rem(y + step, n_y)),
+                src_ref=self.block(total, group),
+                dst_ref=self.target(y),
+                send_sem=out_send.at[self.call],
+                recv_sem=out_recv.at[self.call],
+                device_id=at(sibling if group else gz, lax.rem(y + step, n_y)),
                 device_id_type=MESH,
             )
 
-        def arriving(self, step):
-            from_ = lax.rem(y + n_y - step, n_y)
-            return pltpu.make_async_remote_copy(
-                src_ref=self.block(total, self.call, core),
-                dst_ref=result.at[self.call, pl.ds(0, self.sums), :, self.rows(from_)],
-                send_sem=out_send.at[self.call, core, step],
-                recv_sem=out_recv.at[self.call, step],
-                device_id=at(),
-                device_id_type=MESH,
-            )
-
         def send(self):
-            for step in range(1, n_y):
-                self.gather(step, core).start()
+            for step in SPREAD:
+                self.gather(step).start()
 
             @pl.when(jnp.logical_not(reducer))
             def _():
-                self.gather(0, core).start()
+                self.gather(0).start()
 
         def reduce(self):
             @pl.when(reducer)
             def _():
-                self.block(parts, self.call, core, 0)[...] = self.source(y)[...]
-                self.gather(0, 1 - core).wait_recv()
-                for step in range(1, n_y):
-                    for c in range(2):
-                        self.gather(step, c).wait_recv()
-                for c in range(2):
-                    block = self.block(parts, self.call, c, 0)[...]
+                own = self.source(y)[...]
+                self.wait(self.seven(), in_recv.at[self.call], True)
+                for group in range(2):
+                    block = self.block(parts, n_y)[...] if group else own
                     for step in range(1, n_y):
-                        block = block + self.block(parts, self.call, c, step)[...]
-                    self.block(half_sum, self.call, c)[...] = block
+                        block = block + self.block(parts, group * n_y + step)[...]
+                    self.block(half_sum, group)[...] = block
                 self.swap().start()
 
         def finish(self):
             @pl.when(reducer)
             def _():
                 self.swap().wait_recv()
-                for c in range(2):
-                    self.block(total, self.call, c)[...] = (
-                        self.block(half_sum, self.call, c)[...] + self.block(half_in, self.call, c)[...]
-                    )
-                for step in range(1, n_y):
-                    for c in range(2):
-                        self.spread(step, c).start()
-                self.spread(0, 1 - core).start()
-                result[self.call, pl.ds(0, self.sums), :, self.rows(y)] = self.block(total, self.call, core)[...]
+                for group in range(2):
+                    block = self.block(half_sum, group)[...] + self.block(half_in, 1 - group)[...]
+                    self.block(total, group)[...] = block
+                    if group == 0:
+                        self.target(y)[...] = block
+                for step in SPREAD:
+                    for group in range(2):
+                        self.spread(step, group).start()
+                self.spread(0, 1).start()
 
         def arrive(self):
-            for step in range(1, n_y):
-                self.arriving(step).wait_recv()
-
-            @pl.when(jnp.logical_not(reducer))
-            def _():
-                self.arriving(0).wait_recv()
+            for others, count in ((reducer, n_y - 1), (jnp.logical_not(reducer), n_y)):
+
+                @pl.when(others)
+                def _():
+                    self.wait(self.target(0, count), out_recv.at[self.call], True)
 
         def drain(self):
-            for step in range(1, n_y):
-                self.gather(step, core).wait_send()
-
-            @pl.when(jnp.logical_not(reducer))
-            def _():
-                self.gather(0, core).wait_send()
+            for others, count in ((reducer, n_y - 1), (jnp.logical_not(reducer), n_y)):
+
+                @pl.when(others)
+                def _():
+                    self.wait(self.source(0, count), in_send.at[self.call], False)
 
             @pl.when(reducer)
             def _():
                 self.swap().wait_send()
-                for step in range(1, n_y):
-                    for c in range(2):
-                        self.spread(step, c).wait_send()
-                self.spread(0, 1 - core).wait_send()
+                self.wait(self.seven(), out_send.at[self.call], False)
 
     squares_first = Total(0, 1, 0, nx)
     second = [Total(1 + h, 2, h * half_rows, half_rows) for h in range(HALVES)]
@@ -229,8 +221,6 @@
         return 0
 
     lax.fori_loop(0, order * planes, own_middle, 0)
-    squares_first.reduce()
-
     loads[1].wait()
 
     def own_adjoint(i, _):
@@ -240,13 +230,14 @@
         adj[p, z] = (1.0 + m) * value + (m * k) * flat_laplacian(value, a[p, 1 - z])
         return 0
 
-    lax.fori_loop(0, order * planes, own_adjoint, 0)
+    lax.fori_loop(0, order, own_adjoint, 0)
+    squares_first.reduce()
+    lax.fori_loop(order, order * planes, own_adjoint, 0)
     squares_first.finish()
     squares_first.arrive()
     squares_first.drain()
 
-    u_near.wait_recv()
-    for h in range(HALVES):
+    def middle_half(h):
         rows = half(h)
         u_far[h].wait_recv()
         for z in range(planes):
@@ -265,13 +256,8 @@
             partial[0, z, rows] = squares
             partial[1, z, rows] = coupled
         second[h].send()
-        second[h].reduce()
-        second[h].finish()
-        second[h].arrive()
-        second[h].drain()
-
-    a_near.wait_recv()
-    for h in range(HALVES):
+
+    def adjoint_half(h):
         rows = half(h)
         a_far[h].wait_recv()
         for z in range(planes):
@@ -295,8 +281,21 @@
         w_near[h].start()
         coupled_first[h].send()
 
-    for h in range(HALVES):
-        coupled_first[h].reduce()
+    u_near.wait_recv()
+    middle_half(0)
+    second[0].reduce()
+    middle_half(1)
+    second[0].finish()
+    second[1].reduce()
+    second[0].arrive()
+    second[0].drain()
+    second[1].finish()
+    a_near.wait_recv()
+    adjoint_half(0)
+    second[1].arrive()
+    second[1].drain()
+    coupled_first[0].reduce()
+    adjoint_half(1)
 
     def own_result(i, _):
         p, z = i // planes, lax.rem(i, planes)
@@ -306,9 +305,11 @@
         adj[p, z] = local + stiff[p] * flat_laplacian(scaled, w[p, 1 - z])
         return 0
 
-    lax.fori_loop(0, order * planes, own_result, 0)
-    for h in range(HALVES):
-        coupled_first[h].finish()
+    coupled_first[0].finish()
+    lax.fori_loop(0, order, own_result, 0)
+    coupled_first[1].reduce()
+    lax.fori_loop(order, order * planes, own_result, 0)
+    coupled_first[1].finish()
     for h in range(HALVES):
         rows = half(h)
         coupled_first[h].arrive()
@@ -348,7 +349,7 @@
         + [pltpu.VMEM(shape, f32)] * 7
         + [
             pltpu.VMEM((2, planes, nx, ny), f32),
-            pltpu.VMEM((calls, 2, n_y, 2, planes, quarter, ny), f32),
+            pltpu.VMEM((calls, 2 * n_y, 2, planes, quarter, ny), f32),
             pltpu.VMEM((calls, 2, 2, planes, quarter, ny), f32),
             pltpu.VMEM((calls, 2, 2, planes, quarter, ny), f32),
             pltpu.VMEM((calls, 2, 2, planes, quarter, ny), f32),
@@ -358,12 +359,9 @@
             pltpu.SemaphoreType.DMA((3 * HALVES,)),
             pltpu.SemaphoreType.DMA((2 + HALVES,)),
             pltpu.SemaphoreType.DMA((2 + HALVES,)),
-            pltpu.SemaphoreType.DMA((calls, n_y)),
-            pltpu.SemaphoreType.DMA((calls, 2, n_y)),
-            pltpu.SemaphoreType.DMA((calls,)),
-            pltpu.SemaphoreType.DMA((calls,)),
-            pltpu.SemaphoreType.DMA((calls, 2, n_y)),
-            pltpu.SemaphoreType.DMA((calls, n_y)),
+        ]
+        + [pltpu.SemaphoreType.DMA((calls,))] * 6
+        + [
             pltpu.SemaphoreType.DMA,
         ],
         compiler_params=pltpu.CompilerParams(

time: 77.9 us -> 70.4 us (0.904); the launches traced: 77.8 us -> 69.5 us
  Pallas kernels: 76.3 us -> 67.9 us
    pallas_call x1, Pallas kernels: 76.3 us -> 67.9 us  [on_device(): pl.pallas_call(functools.partial(kernel, n_gz, n_y), out_shape=(field, fi...]
where the time goes in v2:
time: 70.4 us; the launch traced here: 69.5 us
  Pallas kernels  67.9 us (96%)
  other arithmetic  1.49 us (2%)
    pallas_call x1, Pallas kernels, on_device(): pl.pallas_call(functools.partial(kernel, n_gz, n_y), out_shape=(field, fi...  67.9 us
    add x1, other arithmetic, on_device(): return part + stiffness.reshape(-1, 1, 1, 1) * w_halo  1.49 us

profile of v2, /device:TPU:32, one launch (start us, length us, event | category | flops | bytes accessed | tf_op | source)
XLA Modules:
  0.0 69.5 jit_solution(6715162974823978760)
XLA Ops:
  0.0 0.0 copy-start
  0.0 67.9 %adjoint_steps.1 = (f32[12,2,128,128]{3,2,1,0:T(8,128)S(1)}, f32[12,2,128,128]{3,2,1,0:T(8,128)S(1)}) custom-call(f32[12,2,128,128]{3,2,1,0:T(8,128)} %u_hbm.1, f32[12,2,128,128]{3,2,1,0:T(8,128)} %a_hbm.1, f32[12]{0:T(128)} %rate_hbm.1, f32[12]{0:T(128)} %stiff_hbm.1), custom_call_target="tpu_custom_call" | custom-call | tf_op jit(solution)/shard_map/adjoint_steps/pallas_call | solution.py:343
  68.0 0.0 copy-done
  68.0 1.5 %multiply_add_fusion = f32[12,2,128,128]{3,2,1,0:T(8,128)} fusion(f32[12,2,128,128]{3,2,1,0:T(8,128)S(1)} %get-tuple-element.7, f32[12,2,128,128]{3,2,1,0:T(8,128)S(1)} %get-tuple-element.8, f32[12]{0:T(128)S(1)} %copy-done), kind=kLoop, calls=%fused_computation | loop fusion | flops 786432 | bytes 4718640 | tf_op jit(solution)/shard_map/add | solution.py:372
Async XLA Ops:
  0.0 68.0 %copy-start = (f32[12]{0:T(128)S(1)}, f32[12]{0:T(128)}, u32[]{:S(2)}) copy-start(f32[12]{0:T(128)} %stiff_hbm.1) | copy-start | bytes 148

commit v3 on v2

--- a/solution.py
+++ b/solution.py
@@ -28,7 +28,7 @@
     part, w_halo,
     rate, stiff, u, a, mid, adj, w, u_halo, a_halo, partial, parts, half_sum, half_in, total, result,
     load_sem, far_send, far_recv, near_send, near_recv,
-    in_send, in_recv, mid_send, mid_recv, out_send, out_recv, store_sem,
+    in_send, in_recv, mid_send, mid_recv, out_send, out_recv, store_sem, turn,
 ):
     order, planes, nx, ny = u.shape
     gz, ord_ = lax.axis_index("gz"), lax.axis_index("ord")
@@ -55,7 +55,7 @@
         copy.start()
 
     barrier = pltpu.get_barrier_semaphore()
-    peers = [at(far), at(sibling, zl_=1 - zl), at(sibling)]
+    peers = [at(far), at(sibling, zl_=1 - zl), at(sibling), at(zl_=1 - zl)]
     for step in range(1, n_y):
         for c in range(2):
             peers.append(at(chip + c, lax.rem(y + step, n_y)))
@@ -84,8 +84,17 @@
     u_near = halo(0, u_hbm, u_halo, False, pl.ds(0, nx))
     a_near = halo(1, a_hbm, a_halo, False, pl.ds(0, nx))
     w_near = [halo(2 + h, w, w_halo, False, half(h)) for h in range(HALVES)]
-    for copy in u_far + [u_near] + a_far:
+    for copy in u_far + [u_near]:
         copy.start()
+
+    a_far[0].start()
+
+    def yield_link():
+        for copy in u_far:
+            copy.wait_send()
+        pl.semaphore_signal(turn, inc=1, device_id=at(zl_=1 - zl), device_id_type=MESH)
+        pl.semaphore_wait(turn, 1)
+        a_far[1].start()
 
     class Total:
         def __init__(self, call, sums, first, rows):
@@ -284,6 +293,7 @@
     u_near.wait_recv()
     middle_half(0)
     second[0].reduce()
+    yield_link()
     middle_half(1)
     second[0].finish()
     second[1].reduce()
@@ -325,7 +335,7 @@
     store.start()
     for h in range(HALVES):
         coupled_first[h].drain()
-    for copy in u_far + a_far + [u_near, a_near]:
+    for copy in a_far + [u_near, a_near]:
         copy.wait_send()
     for copy in w_near + w_far:
         copy.wait()
@@ -363,6 +373,7 @@
         + [pltpu.SemaphoreType.DMA((calls,))] * 6
         + [
             pltpu.SemaphoreType.DMA,
+            pltpu.SemaphoreType.REGULAR,
         ],
         compiler_params=pltpu.CompilerParams(
             collective_id=0, has_side_effects=True, vmem_limit_bytes=32 << 20

time: 70.4 us -> 68.1 us (0.967); the launches traced: 69.5 us -> 68 us
  Pallas kernels: 67.9 us -> 66.5 us
    pallas_call x1, Pallas kernels: 67.9 us -> 66.5 us  [on_device(): pl.pallas_call(functools.partial(kernel, n_gz, n_y), out_shape=(field, fi...]
where the time goes in v3:
time: 68.1 us; the launch traced here: 68 us
  Pallas kernels  66.5 us (98%)
  other arithmetic  1.49 us (2%)
    pallas_call x1, Pallas kernels, on_device(): pl.pallas_call(functools.partial(kernel, n_gz, n_y), out_shape=(field, fi...  66.5 us
    add x1, other arithmetic, on_device(): return part + stiffness.reshape(-1, 1, 1, 1) * w_halo  1.49 us

profile of v3, /device:TPU:32, one launch (start us, length us, event | category | flops | bytes accessed | tf_op | source)
XLA Modules:
  0.0 68.0 jit_solution(1643083344713054248)
XLA Ops:
  0.0 0.0 copy-start
  0.0 66.5 %adjoint_steps.1 = (f32[12,2,128,128]{3,2,1,0:T(8,128)S(1)}, f32[12,2,128,128]{3,2,1,0:T(8,128)S(1)}) custom-call(f32[12,2,128,128]{3,2,1,0:T(8,128)} %u_hbm.1, f32[12,2,128,128]{3,2,1,0:T(8,128)} %a_hbm.1, f32[12]{0:T(128)} %rate_hbm.1, f32[12]{0:T(128)} %stiff_hbm.1), custom_call_target="tpu_custom_call" | custom-call | tf_op jit(solution)/shard_map/adjoint_steps/pallas_call | solution.py:353
  66.5 0.0 copy-done
  66.5 1.5 %multiply_add_fusion = f32[12,2,128,128]{3,2,1,0:T(8,128)} fusion(f32[12,2,128,128]{3,2,1,0:T(8,128)S(1)} %get-tuple-element.7, f32[12,2,128,128]{3,2,1,0:T(8,128)S(1)} %get-tuple-element.8, f32[12]{0:T(128)S(1)} %copy-done), kind=kLoop, calls=%fused_computation | loop fusion | flops 786432 | bytes 4718640 | tf_op jit(solution)/shard_map/add | solution.py:383
Async XLA Ops:
  0.0 66.5 %copy-start = (f32[12]{0:T(128)S(1)}, f32[12]{0:T(128)}, u32[]{:S(2)}) copy-start(f32[12]{0:T(128)} %stiff_hbm.1) | copy-start | bytes 148

commit v4 on v3

--- a/solution.py
+++ b/solution.py
@@ -280,7 +280,7 @@
                 value = value - field * pull + (m * k) * a_halo[p, z, rows]
                 adj[p, z, rows] = value
                 scaled = m * value
-                w[p, z, rows] = scaled
+                w[p, z, rows] = k * scaled
                 return acc + u[p, z, rows] * scaled
 
             partial[0, z, rows] = lax.fori_loop(
@@ -304,21 +304,20 @@
     adjoint_half(0)
     second[1].arrive()
     second[1].drain()
+    adjoint_half(1)
     coupled_first[0].reduce()
-    adjoint_half(1)
 
     def own_result(i, _):
         p, z = i // planes, lax.rem(i, planes)
-        value, scaled = u[p, z], w[p, z]
+        value, full = u[p, z], adj[p, z]
         slope = CUBE * (value * value) + (2.0 * COUPLE) * result[0, 0, z]
-        local = adj[p, z] + scaled - scaled * slope
-        adj[p, z] = local + stiff[p] * flat_laplacian(scaled, w[p, 1 - z])
+        local = full + (rate[p] * full) * (1.0 - slope)
+        adj[p, z] = local + flat_laplacian(w[p, z], w[p, 1 - z])
         return 0
 
+    lax.fori_loop(0, order * planes, own_result, 0)
+    coupled_first[1].reduce()
     coupled_first[0].finish()
-    lax.fori_loop(0, order, own_result, 0)
-    coupled_first[1].reduce()
-    lax.fori_loop(order, order * planes, own_result, 0)
     coupled_first[1].finish()
     for h in range(HALVES):
         rows = half(h)
@@ -340,6 +339,18 @@
     for copy in w_near + w_far:
         copy.wait()
     store.wait()
+
+
+def add_halo(part, w_halo, out, whole, sem):
+    order = whole.shape[0]
+
+    def one(p, _):
+        whole[p] = part[p] + w_halo[p]
+        pltpu.make_async_copy(whole.at[p], out.at[p], sem).start()
+        return 0
+
+    lax.fori_loop(0, order, one, 0)
+    pltpu.make_async_copy(whole, out, sem).wait()
 
 
 def on_device(n_gz, n_ord, initial, cotangent, mobility, stiffness):
@@ -380,7 +391,15 @@
         ),
         name="adjoint_steps",
     )(*(pltpu.with_memory_space_constraint(x, pltpu.HBM) for x in (initial, cotangent, mobility, stiffness)))
-    return part + stiffness.reshape(-1, 1, 1, 1) * w_halo
+    return pl.pallas_call(
+        add_halo,
+        out_shape=field,
+        in_specs=[pl.BlockSpec(memory_space=pltpu.VMEM)] * 2,
+        out_specs=pl.BlockSpec(memory_space=pltpu.HBM),
+        scratch_shapes=[pltpu.VMEM(shape, f32), pltpu.SemaphoreType.DMA],
+        compiler_params=pltpu.CompilerParams(vmem_limit_bytes=16 << 20),
+        name="add_halo",
+    )(part, w_halo)
 
 
 def solution(mesh):

time: 68.1 us -> 66.6 us (0.978); the launches traced: 68 us -> 65.6 us
  other arithmetic: 1.49 us -> 0 us
  Pallas kernels: 66.5 us -> 65.5 us
    pallas_call x1, Pallas kernels: 66.5 us -> 64.4 us  [on_device(): pl.pallas_call(functools.partial(kernel, n_gz, n_y), out_shape=(field, fi...]
    add x1 -> x0, other arithmetic: 1.49 us -> none  [on_device(): return part + stiffness.reshape(-1, 1, 1, 1) * w_halo]
    pallas_call x0 -> x1, Pallas kernels: none -> 1.15 us  [on_device(): pl.pallas_call(add_halo, out_shape=field, in_specs=[pl.BlockSpec(memory_s...]
where the time goes in v4:
time: 66.6 us; the launch traced here: 65.6 us
  Pallas kernels  65.5 us (98%)
    pallas_call x1, Pallas kernels, on_device(): pl.pallas_call(functools.partial(kernel, n_gz, n_y), out_shape=(field, fi...  64.4 us

profile of v4, /device:TPU:32, one launch (start us, length us, event | category | flops | bytes accessed | tf_op | source)
XLA Modules:
  0.0 65.6 jit_solution(8446020483510350002)
XLA Ops:
  0.0 64.4 %adjoint_steps.1 = (f32[12,2,128,128]{3,2,1,0:T(8,128)S(1)}, f32[12,2,128,128]{3,2,1,0:T(8,128)S(1)}) custom-call(f32[12,2,128,128]{3,2,1,0:T(8,128)} %u_hbm.1, f32[12,2,128,128]{3,2,1,0:T(8,128)} %a_hbm.1, f32[12]{0:T(128)} %rate_hbm.1, f32[12]{0:T(128)} %stiff_hbm.1), custom_call_target="tpu_custom_call" | custom-call | tf_op jit(solution)/shard_map/adjoint_steps/pallas_call | solution.py:364
  64.4 1.1 %add_halo.1 = f32[12,2,128,128]{3,2,1,0:T(8,128)} custom-call(f32[12,2,128,128]{3,2,1,0:T(8,128)S(1)} %get-tuple-element.7.part, f32[12,2,128,128]{3,2,1,0:T(8,128)S(1)} %get-tuple-element.8.w_halo), custom_call_target="tpu_custom_call" | custom-call | tf_op jit(solution)/shard_map/add_halo/pallas_call | solution.py:394

commit v5 on v4

--- a/solution.py
+++ b/solution.py
@@ -286,7 +286,10 @@
             partial[0, z, rows] = lax.fori_loop(
                 0, order, adjoint, jnp.zeros((half_rows, ny), jnp.float32)
             )
-        w_far[h].start()
+        if h == 0:
+            w_far[0].start()
+        else:
+            pl.when(jnp.logical_not(reducer))(w_far[1].start)
         w_near[h].start()
         coupled_first[h].send()
 
@@ -317,6 +320,17 @@
 
     lax.fori_loop(0, order * planes, own_result, 0)
     coupled_first[1].reduce()
+
+    @pl.when(reducer)
+    def _():
+        pl.semaphore_wait(turn, 1)
+        w_far[1].start()
+
+    @pl.when(jnp.logical_not(reducer))
+    def _():
+        w_far[0].wait_send()
+        pl.semaphore_signal(turn, inc=1, device_id=at(zl_=1 - zl), device_id_type=MESH)
+
     coupled_first[0].finish()
     coupled_first[1].finish()
     for h in range(HALVES):
@@ -336,8 +350,13 @@
         coupled_first[h].drain()
     for copy in a_far + [u_near, a_near]:
         copy.wait_send()
-    for copy in w_near + w_far:
+    for copy in w_near + [w_far[1]]:
         copy.wait()
+    w_far[0].wait_recv()
+
+    @pl.when(reducer)
+    def _():
+        w_far[0].wait_send()
     store.wait()
 
 

time: 66.6 us -> 66 us (level)
  no operation moved by 1% of the time
where the time goes in v5:
time: 66 us; the launch traced here: 65.6 us
  Pallas kernels  65.6 us (99%)
    pallas_call x1, Pallas kernels, on_device(): pl.pallas_call(functools.partial(kernel, n_gz, n_y), out_shape=(field, fi...  64.4 us

profile of v5, /device:TPU:32, one launch (start us, length us, event | category | flops | bytes accessed | tf_op | source)
XLA Modules:
  0.0 65.6 jit_solution(3812956027492096279)
XLA Ops:
  0.0 64.4 %adjoint_steps.1 = (f32[12,2,128,128]{3,2,1,0:T(8,128)S(1)}, f32[12,2,128,128]{3,2,1,0:T(8,128)S(1)}) custom-call(f32[12,2,128,128]{3,2,1,0:T(8,128)} %u_hbm.1, f32[12,2,128,128]{3,2,1,0:T(8,128)} %a_hbm.1, f32[12]{0:T(128)} %rate_hbm.1, f32[12]{0:T(128)} %stiff_hbm.1), custom_call_target="tpu_custom_call" | custom-call | tf_op jit(solution)/shard_map/adjoint_steps/pallas_call | solution.py:383
  64.4 1.1 %add_halo.1 = f32[12,2,128,128]{3,2,1,0:T(8,128)} custom-call(f32[12,2,128,128]{3,2,1,0:T(8,128)S(1)} %get-tuple-element.7.part, f32[12,2,128,128]{3,2,1,0:T(8,128)S(1)} %get-tuple-element.8.w_halo), custom_call_target="tpu_custom_call" | custom-call | tf_op jit(solution)/shard_map/add_halo/pallas_call | solution.py:413

commit v6 on v5

--- a/solution.py
+++ b/solution.py
@@ -124,8 +124,8 @@
             return pltpu.make_async_remote_copy(
                 src_ref=self.source(to),
                 dst_ref=self.block(parts, jnp.where(reducer, 0, n_y) + step),
-                send_sem=in_send.at[self.call],
-                recv_sem=in_recv.at[self.call],
+                send_sem=in_send.at[self.call % 3],
+                recv_sem=in_recv.at[self.call % 3],
                 device_id=at(chip + zl, to),
                 device_id_type=MESH,
             )
@@ -134,8 +134,8 @@
             return pltpu.make_async_remote_copy(
                 src_ref=self.block(half_sum, slice(None)),
                 dst_ref=self.block(half_in, slice(None)),
-                send_sem=mid_send.at[self.call],
-                recv_sem=mid_recv.at[self.call],
+                send_sem=mid_send.at[self.call % 3],
+                recv_sem=mid_recv.at[self.call % 3],
                 device_id=at(sibling, zl_=1 - zl),
                 device_id_type=MESH,
             )
@@ -144,8 +144,8 @@
             return pltpu.make_async_remote_copy(
                 src_ref=self.block(total, group),
                 dst_ref=self.target(y),
-                send_sem=out_send.at[self.call],
-                recv_sem=out_recv.at[self.call],
+                send_sem=out_send.at[self.call % 3],
+                recv_sem=out_recv.at[self.call % 3],
                 device_id=at(sibling if group else gz, lax.rem(y + step, n_y)),
                 device_id_type=MESH,
             )
@@ -162,7 +162,7 @@
             @pl.when(reducer)
             def _():
                 own = self.source(y)[...]
-                self.wait(self.seven(), in_recv.at[self.call], True)
+                self.wait(self.seven(), in_recv.at[self.call % 3], True)
                 for group in range(2):
                     block = self.block(parts, n_y)[...] if group else own
                     for step in range(1, n_y):
@@ -189,19 +189,19 @@
 
                 @pl.when(others)
                 def _():
-                    self.wait(self.target(0, count), out_recv.at[self.call], True)
+                    self.wait(self.target(0, count), out_recv.at[self.call % 3], True)
 
         def drain(self):
             for others, count in ((reducer, n_y - 1), (jnp.logical_not(reducer), n_y)):
 
                 @pl.when(others)
                 def _():
-                    self.wait(self.source(0, count), in_send.at[self.call], False)
+                    self.wait(self.source(0, count), in_send.at[self.call % 3], False)
 
             @pl.when(reducer)
             def _():
                 self.swap().wait_send()
-                self.wait(self.seven(), out_send.at[self.call], False)
+                self.wait(self.seven(), out_send.at[self.call % 3], False)
 
     squares_first = Total(0, 1, 0, nx)
     second = [Total(1 + h, 2, h * half_rows, half_rows) for h in range(HALVES)]
@@ -400,7 +400,7 @@
             pltpu.SemaphoreType.DMA((2 + HALVES,)),
             pltpu.SemaphoreType.DMA((2 + HALVES,)),
         ]
-        + [pltpu.SemaphoreType.DMA((calls,))] * 6
+        + [pltpu.SemaphoreType.DMA((3,))] * 6
         + [
             pltpu.SemaphoreType.DMA,
             pltpu.SemaphoreType.REGULAR,

time: 66 us -> 65.9 us (level)
  no operation moved by 1% of the time
where the time goes in v6:
time: 65.9 us; the launch traced here: 65.5 us
  Pallas kernels  65.5 us (99%)
    pallas_call x1, Pallas kernels, on_device(): pl.pallas_call(functools.partial(kernel, n_gz, n_y), out_shape=(field, fi...  64.3 us

profile of v6, /device:TPU:32, one launch (start us, length us, event | category | flops | bytes accessed | tf_op | source)
XLA Modules:
  0.0 65.5 jit_solution(5772435240847518474)
XLA Ops:
  0.0 64.3 %adjoint_steps.1 = (f32[12,2,128,128]{3,2,1,0:T(8,128)S(1)}, f32[12,2,128,128]{3,2,1,0:T(8,128)S(1)}) custom-call(f32[12,2,128,128]{3,2,1,0:T(8,128)} %u_hbm.1, f32[12,2,128,128]{3,2,1,0:T(8,128)} %a_hbm.1, f32[12]{0:T(128)} %rate_hbm.1, f32[12]{0:T(128)} %stiff_hbm.1), custom_call_target="tpu_custom_call" | custom-call | tf_op jit(solution)/shard_map/adjoint_steps/pallas_call | solution.py:383
  64.3 1.1 %add_halo.1 = f32[12,2,128,128]{3,2,1,0:T(8,128)} custom-call(f32[12,2,128,128]{3,2,1,0:T(8,128)S(1)} %get-tuple-element.7.part, f32[12,2,128,128]{3,2,1,0:T(8,128)S(1)} %get-tuple-element.8.w_halo), custom_call_target="tpu_custom_call" | custom-call | tf_op jit(solution)/shard_map/add_halo/pallas_call | solution.py:413

commit v7 on v6

--- a/solution.py
+++ b/solution.py
@@ -343,7 +343,7 @@
                 adj[p, z, rows] = adj[p, z, rows] - u[p, z, rows] * pull
                 return 0
 
-            lax.fori_loop(0, order, couple, 0)
+            lax.fori_loop(0, order, couple, 0, unroll=2)
     store = pltpu.make_async_copy(adj, part, store_sem)
     store.start()
     for h in range(HALVES):
@@ -368,7 +368,7 @@
         pltpu.make_async_copy(whole.at[p], out.at[p], sem).start()
         return 0
 
-    lax.fori_loop(0, order, one, 0)
+    lax.fori_loop(0, order, one, 0, unroll=True)
     pltpu.make_async_copy(whole, out, sem).wait()
 
 

time: 65.9 us -> 65.9 us (level)
  no operation moved by 1% of the time
where the time goes in v7:
time: 65.9 us; the launch traced here: 65.5 us
  Pallas kernels  65.5 us (99%)
    pallas_call x1, Pallas kernels, on_device(): pl.pallas_call(functools.partial(kernel, n_gz, n_y), out_shape=(field, fi...  64.3 us

profile of v7, /device:TPU:32, one launch (start us, length us, event | category | flops | bytes accessed | tf_op | source)
XLA Modules:
  0.0 65.5 jit_solution(6287327459347783774)
XLA Ops:
  0.0 64.3 %adjoint_steps.1 = (f32[12,2,128,128]{3,2,1,0:T(8,128)S(1)}, f32[12,2,128,128]{3,2,1,0:T(8,128)S(1)}) custom-call(f32[12,2,128,128]{3,2,1,0:T(8,128)} %u_hbm.1, f32[12,2,128,128]{3,2,1,0:T(8,128)} %a_hbm.1, f32[12]{0:T(128)} %rate_hbm.1, f32[12]{0:T(128)} %stiff_hbm.1), custom_call_target="tpu_custom_call" | custom-call | tf_op jit(solution)/shard_map/adjoint_steps/pallas_call | solution.py:383
  64.3 1.1 %add_halo.1 = f32[12,2,128,128]{3,2,1,0:T(8,128)} custom-call(f32[12,2,128,128]{3,2,1,0:T(8,128)S(1)} %get-tuple-element.7.part, f32[12,2,128,128]{3,2,1,0:T(8,128)S(1)} %get-tuple-element.8.w_halo), custom_call_target="tpu_custom_call" | custom-call | tf_op jit(solution)/shard_map/add_halo/pallas_call | solution.py:413
